TPU v7x, 32 devices: a whole 2x2x4 slice. The times are simulated.
32 devices in a mesh: depth: 4 (over z), imx: 4 (over y, x), imy: 2 (over core).
Axes of the slice: x: 2, y: 2, z: 4, core: 2. Of those that a mesh axis runs over, the one named last changes fastest.
Arguments:
- field: bfloat16 [128, 256, 512], P('depth', 'imy', 'imx'), may hold values from -6 to 6
- brick_live: int32 [4, 8, 16], P('depth', 'imy', 'imx'), may hold values from 0 to 1, as said below
- order: int32 [32, 64], P('imy', 'imx'), may hold values 0 or 1
- centers: float32 [4], replicated, may hold values from -2 to 2
- widths: float32 [4], replicated, may hold values from 0.3 to 1.2
- heights: float32 [4], replicated, may hold values from 0.5 to 3
- colours: float32 [4, 3], replicated, may hold values from 0.1 to 1
Outputs:
- colour: float32 [3, 256, 512], P(None, ('imy', 'depth'), 'imx')
- logtrans: float32 [256, 512], P(('imy', 'depth'), 'imx')
Inputs may be any that keep to these rules, and one draw needn't show every extreme that they name: `brick_live`: each device's 16 bricks (one slab, 4 bricks along the rows by 4 along the columns) hold between 1 and 16 live bricks; at least one device has all 16 live, and most have few.
All inputs are finite; a program needn't handle non-finite values. No bound on the sum of `order` on one device may be relied on, other than what follows from the above.
Results may differ from a plain program's by a relative error of at most 0.00038.
Values may be sent and summed in bfloat16 or wider, within the bound.
A program may use at most 64 MiB of HBM per device.

v0:
```python
import jax
import jax.numpy as jnp
from jax import lax
from jax.sharding import PartitionSpec as P

OPTICAL = 3.0


def padded_2(value, sides, width):
    for axis, dim in sides:
        count, length = (lax.axis_size(axis), value.shape[dim])
        up = [(i, (i + 1) % count) for i in range(count - 1)]
        down = [(j, i) for i, j in up]
        last = lax.slice_in_dim(value, length - width, length, axis=dim)
        initial = lax.slice_in_dim(value, 0, width, axis=dim)
        before = lax.ppermute(last, axis, up)
        after = lax.ppermute(initial, axis, down)
        value = jnp.concatenate([before, value, after], axis=dim)
    return value


def from_partner(block, axis, distance):
    count = lax.axis_size(axis)
    route = []
    for low in range(count):
        high = low | 1 << distance
        if high != low and high < count:
            route += [(low, high), (high, low)]
    return lax.ppermute(block, axis, route)


def shade_cells(padded):
    grad_z = (padded[2:, 1:-1, 1:-1] - padded[:-2, 1:-1, 1:-1]) * 0.5
    grad_x = (padded[1:-1, 2:, 1:-1] - padded[1:-1, :-2, 1:-1]) * 0.5
    grad_y = (padded[1:-1, 1:-1, 2:] - padded[1:-1, 1:-1, :-2]) * 0.5
    facing = grad_z * 0.64 + grad_x * 0.48 + grad_y * 0.6
    length = lax.rsqrt(grad_z * grad_z + grad_x * grad_x + grad_y * grad_y + 1.0)
    return (0.3 + 0.7 * jnp.abs(facing) * length).astype(jnp.bfloat16)


def render_cells(values, shade, backward, live, centers, widths, heights, colours, step_len):
    valf = values.astype(jnp.float32)
    sigma = jnp.zeros(valf.shape, jnp.float32)
    emits = [jnp.zeros(valf.shape, jnp.float32) for chan in range(3)]
    for bumpno in range(centers.shape[0]):
        bump = jnp.exp(-0.5 * jnp.square((valf - centers[bumpno]) / widths[bumpno]))
        sigma = sigma + heights[bumpno] * bump
        emits = [emits[chan] + colours[bumpno, chan] * bump for chan in range(3)]
    tau = sigma * (step_len * live)
    absorb = -jnp.expm1(-tau)
    running = jnp.cumsum(tau, axis=0)
    total = running[-1]
    before = jnp.where(backward, total - running, running - tau)
    weight = jnp.exp(-before) * absorb * shade.astype(jnp.float32)
    parts = [jnp.sum(weight * emits[chan], axis=0) for chan in range(3)]
    return jnp.stack(parts + [-total])


def over_pair(lower, upper, backward):
    front = jnp.where(backward, upper, lower)
    behind = jnp.where(backward, lower, upper)
    mixed = front[:3] + jnp.exp(front[3]) * behind[:3]
    return jnp.concatenate([mixed, (front[3] + behind[3])[None]], axis=0)


def local(field, brick_live, order, centers, widths, heights, colours):
    depth_count = lax.axis_size("depth")
    zdev, xdev, ydev = field.shape
    step_len = OPTICAL / (zdev * depth_count)
    padded = padded_2(field, (("depth", 0), ("imx", 2), ("imy", 1)), 1)
    shade = shade_cells(padded.astype(jnp.float32))
    tile_side = xdev // order.shape[0]
    backward = jnp.repeat(jnp.repeat(order, tile_side, axis=0), tile_side, axis=1) == 1
    across = brick_live.shape[2]
    side = xdev // brick_live.shape[1]
    live = brick_live[0].reshape(-1)
    nbricks = live.shape[0]
    listing = jnp.argsort((1 - live) * nbricks + jnp.arange(nbricks, dtype=jnp.int32), stable=True)
    count = jnp.sum(live)
    anchor = jnp.int32(0)

    def corner(slot):
        which = listing[jnp.clip(slot, 0, nbricks - 1)]
        return (which // across * side, which % across * side)

    def cut_brick(row, col):
        vals = lax.dynamic_slice(field, (anchor, row, col), (zdev, side, side))
        shades = lax.dynamic_slice(shade, (anchor, row, col), (zdev, side, side))
        marks = lax.dynamic_slice(backward, (row, col), (side, side))
        return (vals, shades, marks)

    def draw_brick(vals, shades, marks):
        return render_cells(vals, shades, marks, 1.0, centers, widths, heights, colours, step_len)

    def paint(slot, image):
        row, col = corner(slot)
        piece = draw_brick(*cut_brick(row, col))
        return lax.dynamic_update_slice(image, piece, (anchor, row, col))

    image = jnp.zeros((4, xdev, ydev), jnp.float32)
    levels = depth_count.bit_length() - 1
    counts_all = lax.all_gather(count.reshape(1), "depth", axis=0, tiled=True)
    myself = lax.axis_index("depth")
    members = jnp.arange(depth_count, dtype=jnp.int32)
    loads = counts_all
    handed = jnp.zeros((depth_count,), jnp.int32)
    plan = []
    for level in range(levels):
        pair_ids = jnp.bitwise_xor(members, 1 << level)
        partner_load = loads[pair_ids]
        giving = ((loads - partner_load >= 2) & (counts_all - handed >= 2)).astype(jnp.int32)
        taking = giving[pair_ids]
        plan.append((giving[myself], taking[myself], counts_all[myself] - 1 - handed[myself]))
        loads = loads - giving + taking
        handed = handed + giving
    image = lax.fori_loop(0, count - handed[myself], paint, image)
    for level in range(levels):
        gives, takes, slot = plan[level]
        used = gives > 0
        pack_row, pack_col = corner(slot)
        pack_vals, pack_shades, pack_marks = cut_brick(pack_row, pack_col)
        stacked = jnp.stack([pack_vals, pack_shades])
        pack_marks = pack_marks.astype(jnp.bfloat16)
        sent_vals = jnp.where(used, stacked, jnp.zeros_like(stacked))
        sent_marks = jnp.where(used, pack_marks, jnp.zeros_like(pack_marks))
        got_vals, got_marks = from_partner((sent_vals, sent_marks), "depth", level)

        def render_taken(vals, marks):
            return draw_brick(vals[0], vals[1], marks > 0.5)

        def render_none(vals, marks):
            return jnp.zeros((4, side, side), jnp.float32)

        piece = lax.cond(takes > 0, render_taken, render_none, got_vals, got_marks)
        back = from_partner(piece, "depth", level)
        place_row, place_col = corner(slot)
        place_current = lax.dynamic_slice(image, (anchor, place_row, place_col), (4, side, side))
        image = lax.dynamic_update_slice(
            image, jnp.where(used, back, place_current), (anchor, place_row, place_col)
        )
    rows_out = xdev // depth_count
    levels = depth_count.bit_length() - 1
    position_depth = lax.axis_index("depth")
    current = image.reshape(4, depth_count, rows_out, ydev)
    marks_now = backward.reshape(depth_count, rows_out, ydev)
    for level in range(levels):
        groups = current.shape[1] // 2
        current = current.reshape(4, groups, 2, rows_out, ydev)
        marks_now = marks_now.reshape(groups, 2, rows_out, ydev)
        bit = position_depth >> level & 1
        mine = lax.dynamic_index_in_dim(current, bit, 2, keepdims=False)
        other = lax.dynamic_index_in_dim(current, 1 - bit, 2, keepdims=False)
        marks_now = lax.dynamic_index_in_dim(marks_now, bit, 1, keepdims=False)
        received = from_partner(other, "depth", level)
        lower = jnp.where(bit == 0, mine, received)
        upper = jnp.where(bit == 0, received, mine)
        current = over_pair(lower, upper, marks_now)
    final = current[:, 0]
    return (final[:3], final[3])


def solution(mesh):
    return jax.shard_map(
        local,
        mesh=mesh,
        in_specs=(
            P("depth", "imy", "imx"),
            P("depth", "imy", "imx"),
            P("imy", "imx"),
            P(),
            P(),
            P(),
            P(),
        ),
        out_specs=(P(None, ("imy", "depth"), "imx"), P(("imy", "depth"), "imx")),
        check_vma=False,
    )
```

profile of v0, /device:TPU:18, one launch (start us, length us, event | category | flops | bytes accessed | tf_op | source)
XLA Modules:
  0.0 819.6 jit_solution(17402488395901540503)
XLA Ops:
  75.9 48.1 %collective-permute-start.8 = (f32[4,32,32]{2,1,0:T(8,128)}, f32[4,32,32]{2,1,0:T(8,128)S(1)}, u32[]{:S(2)}, u32[]{:S(2)}) collective-permute-start(f32[4,32,32]{2,1,0:T(8,128)} %get-tuple-element.602), channel_id=1, source_target_pairs={{0,8},{8,0},{16,24},{24,16},{1,9},{9,1},{17,25},{25,17},{2,10},{10... | collective-permute-start | bytes 49160 | tf_op jit(solution)/shard_map/ppermute | solution.py:29
  124.0 676.5 %while.12 = (s32[]{:T(128)}, f32[4,128,128]{2,1,0:T(8,128)S(1)}, s32[]{:T(128)}, s32[16]{0:T(128)S(1)}, pred[128,128]{0,1:T(8,128)(4,1)S(1)}, /*index=5*/f32[4]{...) while((s32[]{:T(128)}, f32[4,128,128]{2,1,0:T(8,128)S(1)}, ...), condition=%wide.region_7.8_spmd, body=%wide.region_2.7_spmd.sunk | while | flops 6072351 | bytes 1290192 | solution.py:116
  137.4 11.2 %multiply_reduce_fusion.6 = f32[32,32]{1,0:T(8,128)S(1)} fusion(f32[]{:T(128)} %bitcast.276, f32[]{:T(128)} %bitcast.277, f32[]{:T(128)} %bitcast.278, f32[]{:T(128)} %bitcast.279, bf16[32,128,128]{2,1,0:T(8,128)(2,1)S(1)} %get-tuple-element.591, s32[]{:T(128)S(6)} %select_n.395, s32[]{:T(128)S(6)} %select_n.397, f32[32,32,32]{2,1,0:T(8,128)S(1)} %fusion.133, ...), kind=kLoop, calls=%fused_computation.24.clone.1 | loop fusion | flops 1408000 | bytes 271432 | tf_op jit(solution)/shard_map/while/body/reduce_sum | solution.py:55
  148.6 11.1 %multiply_reduce_fusion.7 = f32[32,32]{1,0:T(8,128)S(1)} fusion(f32[]{:T(128)} %bitcast.281, f32[]{:T(128)} %bitcast.282, f32[]{:T(128)} %bitcast.283, f32[]{:T(128)} %bitcast.284, bf16[32,128,128]{2,1,0:T(8,128)(2,1)S(1)} %get-tuple-element.591, s32[]{:T(128)S(6)} %select_n.395, s32[]{:T(128)S(6)} %select_n.397, f32[32,32,32]{2,1,0:T(8,128)S(1)} %fusion.133, ...), kind=kLoop, calls=%fused_computation.25.clone.1 | loop fusion | flops 1408000 | bytes 271432 | tf_op jit(solution)/shard_map/while/body/reduce_sum | solution.py:55
  184.9 11.2 %multiply_reduce_fusion.6 = f32[32,32]{1,0:T(8,128)S(1)} fusion(f32[]{:T(128)} %bitcast.276, f32[]{:T(128)} %bitcast.277, f32[]{:T(128)} %bitcast.278, f32[]{:T(128)} %bitcast.279, bf16[32,128,128]{2,1,0:T(8,128)(2,1)S(1)} %get-tuple-element.591, s32[]{:T(128)S(6)} %select_n.395, s32[]{:T(128)S(6)} %select_n.397, f32[32,32,32]{2,1,0:T(8,128)S(1)} %fusion.133, ...), kind=kLoop, calls=%fused_computation.24.clone.1 | loop fusion | flops 1408000 | bytes 271432 | tf_op jit(solution)/shard_map/while/body/reduce_sum | solution.py:55
  196.1 11.1 %multiply_reduce_fusion.7 = f32[32,32]{1,0:T(8,128)S(1)} fusion(f32[]{:T(128)} %bitcast.281, f32[]{:T(128)} %bitcast.282, f32[]{:T(128)} %bitcast.283, f32[]{:T(128)} %bitcast.284, bf16[32,128,128]{2,1,0:T(8,128)(2,1)S(1)} %get-tuple-element.591, s32[]{:T(128)S(6)} %select_n.395, s32[]{:T(128)S(6)} %select_n.397, f32[32,32,32]{2,1,0:T(8,128)S(1)} %fusion.133, ...), kind=kLoop, calls=%fused_computation.25.clone.1 | loop fusion | flops 1408000 | bytes 271432 | tf_op jit(solution)/shard_map/while/body/reduce_sum | solution.py:55
  233.6 11.2 %multiply_reduce_fusion.6 = f32[32,32]{1,0:T(8,128)S(1)} fusion(f32[]{:T(128)} %bitcast.276, f32[]{:T(128)} %bitcast.277, f32[]{:T(128)} %bitcast.278, f32[]{:T(128)} %bitcast.279, bf16[32,128,128]{2,1,0:T(8,128)(2,1)S(1)} %get-tuple-element.591, s32[]{:T(128)S(6)} %select_n.395, s32[]{:T(128)S(6)} %select_n.397, f32[32,32,32]{2,1,0:T(8,128)S(1)} %fusion.133, ...), kind=kLoop, calls=%fused_computation.24.clone.1 | loop fusion | flops 1408000 | bytes 271432 | tf_op jit(solution)/shard_map/while/body/reduce_sum | solution.py:55
  282.2 11.2 %multiply_reduce_fusion.6 = f32[32,32]{1,0:T(8,128)S(1)} fusion(f32[]{:T(128)} %bitcast.276, f32[]{:T(128)} %bitcast.277, f32[]{:T(128)} %bitcast.278, f32[]{:T(128)} %bitcast.279, bf16[32,128,128]{2,1,0:T(8,128)(2,1)S(1)} %get-tuple-element.591, s32[]{:T(128)S(6)} %select_n.395, s32[]{:T(128)S(6)} %select_n.397, f32[32,32,32]{2,1,0:T(8,128)S(1)} %fusion.133, ...), kind=kLoop, calls=%fused_computation.24.clone.1 | loop fusion | flops 1408000 | bytes 271432 | tf_op jit(solution)/shard_map/while/body/reduce_sum | solution.py:55
  330.9 11.2 %multiply_reduce_fusion.6 = f32[32,32]{1,0:T(8,128)S(1)} fusion(f32[]{:T(128)} %bitcast.276, f32[]{:T(128)} %bitcast.277, f32[]{:T(128)} %bitcast.278, f32[]{:T(128)} %bitcast.279, bf16[32,128,128]{2,1,0:T(8,128)(2,1)S(1)} %get-tuple-element.591, s32[]{:T(128)S(6)} %select_n.395, s32[]{:T(128)S(6)} %select_n.397, f32[32,32,32]{2,1,0:T(8,128)S(1)} %fusion.133, ...), kind=kLoop, calls=%fused_computation.24.clone.1 | loop fusion | flops 1408000 | bytes 271432 | tf_op jit(solution)/shard_map/while/body/reduce_sum | solution.py:55
  342.1 11.1 %multiply_reduce_fusion.7 = f32[32,32]{1,0:T(8,128)S(1)} fusion(f32[]{:T(128)} %bitcast.281, f32[]{:T(128)} %bitcast.282, f32[]{:T(128)} %bitcast.283, f32[]{:T(128)} %bitcast.284, bf16[32,128,128]{2,1,0:T(8,128)(2,1)S(1)} %get-tuple-element.591, s32[]{:T(128)S(6)} %select_n.395, s32[]{:T(128)S(6)} %select_n.397, f32[32,32,32]{2,1,0:T(8,128)S(1)} %fusion.133, ...), kind=kLoop, calls=%fused_computation.25.clone.1 | loop fusion | flops 1408000 | bytes 271432 | tf_op jit(solution)/shard_map/while/body/reduce_sum | solution.py:55
  378.4 11.2 %multiply_reduce_fusion.6 = f32[32,32]{1,0:T(8,128)S(1)} fusion(f32[]{:T(128)} %bitcast.276, f32[]{:T(128)} %bitcast.277, f32[]{:T(128)} %bitcast.278, f32[]{:T(128)} %bitcast.279, bf16[32,128,128]{2,1,0:T(8,128)(2,1)S(1)} %get-tuple-element.591, s32[]{:T(128)S(6)} %select_n.395, s32[]{:T(128)S(6)} %select_n.397, f32[32,32,32]{2,1,0:T(8,128)S(1)} %fusion.133, ...), kind=kLoop, calls=%fused_computation.24.clone.1 | loop fusion | flops 1408000 | bytes 271432 | tf_op jit(solution)/shard_map/while/body/reduce_sum | solution.py:55
  389.6 11.1 %multiply_reduce_fusion.7 = f32[32,32]{1,0:T(8,128)S(1)} fusion(f32[]{:T(128)} %bitcast.281, f32[]{:T(128)} %bitcast.282, f32[]{:T(128)} %bitcast.283, f32[]{:T(128)} %bitcast.284, bf16[32,128,128]{2,1,0:T(8,128)(2,1)S(1)} %get-tuple-element.591, s32[]{:T(128)S(6)} %select_n.395, s32[]{:T(128)S(6)} %select_n.397, f32[32,32,32]{2,1,0:T(8,128)S(1)} %fusion.133, ...), kind=kLoop, calls=%fused_computation.25.clone.1 | loop fusion | flops 1408000 | bytes 271432 | tf_op jit(solution)/shard_map/while/body/reduce_sum | solution.py:55
  427.1 11.2 %multiply_reduce_fusion.6 = f32[32,32]{1,0:T(8,128)S(1)} fusion(f32[]{:T(128)} %bitcast.276, f32[]{:T(128)} %bitcast.277, f32[]{:T(128)} %bitcast.278, f32[]{:T(128)} %bitcast.279, bf16[32,128,128]{2,1,0:T(8,128)(2,1)S(1)} %get-tuple-element.591, s32[]{:T(128)S(6)} %select_n.395, s32[]{:T(128)S(6)} %select_n.397, f32[32,32,32]{2,1,0:T(8,128)S(1)} %fusion.133, ...), kind=kLoop, calls=%fused_computation.24.clone.1 | loop fusion | flops 1408000 | bytes 271432 | tf_op jit(solution)/shard_map/while/body/reduce_sum | solution.py:55
  438.3 11.1 %multiply_reduce_fusion.7 = f32[32,32]{1,0:T(8,128)S(1)} fusion(f32[]{:T(128)} %bitcast.281, f32[]{:T(128)} %bitcast.282, f32[]{:T(128)} %bitcast.283, f32[]{:T(128)} %bitcast.284, bf16[32,128,128]{2,1,0:T(8,128)(2,1)S(1)} %get-tuple-element.591, s32[]{:T(128)S(6)} %select_n.395, s32[]{:T(128)S(6)} %select_n.397, f32[32,32,32]{2,1,0:T(8,128)S(1)} %fusion.133, ...), kind=kLoop, calls=%fused_computation.25.clone.1 | loop fusion | flops 1408000 | bytes 271432 | tf_op jit(solution)/shard_map/while/body/reduce_sum | solution.py:55
  475.8 11.2 %multiply_reduce_fusion.6 = f32[32,32]{1,0:T(8,128)S(1)} fusion(f32[]{:T(128)} %bitcast.276, f32[]{:T(128)} %bitcast.277, f32[]{:T(128)} %bitcast.278, f32[]{:T(128)} %bitcast.279, bf16[32,128,128]{2,1,0:T(8,128)(2,1)S(1)} %get-tuple-element.591, s32[]{:T(128)S(6)} %select_n.395, s32[]{:T(128)S(6)} %select_n.397, f32[32,32,32]{2,1,0:T(8,128)S(1)} %fusion.133, ...), kind=kLoop, calls=%fused_computation.24.clone.1 | loop fusion | flops 1408000 | bytes 271432 | tf_op jit(solution)/shard_map/while/body/reduce_sum | solution.py:55
  487.0 11.1 %multiply_reduce_fusion.7 = f32[32,32]{1,0:T(8,128)S(1)} fusion(f32[]{:T(128)} %bitcast.281, f32[]{:T(128)} %bitcast.282, f32[]{:T(128)} %bitcast.283, f32[]{:T(128)} %bitcast.284, bf16[32,128,128]{2,1,0:T(8,128)(2,1)S(1)} %get-tuple-element.591, s32[]{:T(128)S(6)} %select_n.395, s32[]{:T(128)S(6)} %select_n.397, f32[32,32,32]{2,1,0:T(8,128)S(1)} %fusion.133, ...), kind=kLoop, calls=%fused_computation.25.clone.1 | loop fusion | flops 1408000 | bytes 271432 | tf_op jit(solution)/shard_map/while/body/reduce_sum | solution.py:55
  524.4 11.2 %multiply_reduce_fusion.6 = f32[32,32]{1,0:T(8,128)S(1)} fusion(f32[]{:T(128)} %bitcast.276, f32[]{:T(128)} %bitcast.277, f32[]{:T(128)} %bitcast.278, f32[]{:T(128)} %bitcast.279, bf16[32,128,128]{2,1,0:T(8,128)(2,1)S(1)} %get-tuple-element.591, s32[]{:T(128)S(6)} %select_n.395, s32[]{:T(128)S(6)} %select_n.397, f32[32,32,32]{2,1,0:T(8,128)S(1)} %fusion.133, ...), kind=kLoop, calls=%fused_computation.24.clone.1 | loop fusion | flops 1408000 | bytes 271432 | tf_op jit(solution)/shard_map/while/body/reduce_sum | solution.py:55
  571.9 11.2 %multiply_reduce_fusion.6 = f32[32,32]{1,0:T(8,128)S(1)} fusion(f32[]{:T(128)} %bitcast.276, f32[]{:T(128)} %bitcast.277, f32[]{:T(128)} %bitcast.278, f32[]{:T(128)} %bitcast.279, bf16[32,128,128]{2,1,0:T(8,128)(2,1)S(1)} %get-tuple-element.591, s32[]{:T(128)S(6)} %select_n.395, s32[]{:T(128)S(6)} %select_n.397, f32[32,32,32]{2,1,0:T(8,128)S(1)} %fusion.133, ...), kind=kLoop, calls=%fused_computation.24.clone.1 | loop fusion | flops 1408000 | bytes 271432 | tf_op jit(solution)/shard_map/while/body/reduce_sum | solution.py:55
  620.6 11.2 %multiply_reduce_fusion.6 = f32[32,32]{1,0:T(8,128)S(1)} fusion(f32[]{:T(128)} %bitcast.276, f32[]{:T(128)} %bitcast.277, f32[]{:T(128)} %bitcast.278, f32[]{:T(128)} %bitcast.279, bf16[32,128,128]{2,1,0:T(8,128)(2,1)S(1)} %get-tuple-element.591, s32[]{:T(128)S(6)} %select_n.395, s32[]{:T(128)S(6)} %select_n.397, f32[32,32,32]{2,1,0:T(8,128)S(1)} %fusion.133, ...), kind=kLoop, calls=%fused_computation.24.clone.1 | loop fusion | flops 1408000 | bytes 271432 | tf_op jit(solution)/shard_map/while/body/reduce_sum | solution.py:55
  669.3 11.2 %multiply_reduce_fusion.6 = f32[32,32]{1,0:T(8,128)S(1)} fusion(f32[]{:T(128)} %bitcast.276, f32[]{:T(128)} %bitcast.277, f32[]{:T(128)} %bitcast.278, f32[]{:T(128)} %bitcast.279, bf16[32,128,128]{2,1,0:T(8,128)(2,1)S(1)} %get-tuple-element.591, s32[]{:T(128)S(6)} %select_n.395, s32[]{:T(128)S(6)} %select_n.397, f32[32,32,32]{2,1,0:T(8,128)S(1)} %fusion.133, ...), kind=kLoop, calls=%fused_computation.24.clone.1 | loop fusion | flops 1408000 | bytes 271432 | tf_op jit(solution)/shard_map/while/body/reduce_sum | solution.py:55
  717.9 11.2 %multiply_reduce_fusion.6 = f32[32,32]{1,0:T(8,128)S(1)} fusion(f32[]{:T(128)} %bitcast.276, f32[]{:T(128)} %bitcast.277, f32[]{:T(128)} %bitcast.278, f32[]{:T(128)} %bitcast.279, bf16[32,128,128]{2,1,0:T(8,128)(2,1)S(1)} %get-tuple-element.591, s32[]{:T(128)S(6)} %select_n.395, s32[]{:T(128)S(6)} %select_n.397, f32[32,32,32]{2,1,0:T(8,128)S(1)} %fusion.133, ...), kind=kLoop, calls=%fused_computation.24.clone.1 | loop fusion | flops 1408000 | bytes 271432 | tf_op jit(solution)/shard_map/while/body/reduce_sum | solution.py:55
  729.2 11.1 %multiply_reduce_fusion.7 = f32[32,32]{1,0:T(8,128)S(1)} fusion(f32[]{:T(128)} %bitcast.281, f32[]{:T(128)} %bitcast.282, f32[]{:T(128)} %bitcast.283, f32[]{:T(128)} %bitcast.284, bf16[32,128,128]{2,1,0:T(8,128)(2,1)S(1)} %get-tuple-element.591, s32[]{:T(128)S(6)} %select_n.395, s32[]{:T(128)S(6)} %select_n.397, f32[32,32,32]{2,1,0:T(8,128)S(1)} %fusion.133, ...), kind=kLoop, calls=%fused_computation.25.clone.1 | loop fusion | flops 1408000 | bytes 271432 | tf_op jit(solution)/shard_map/while/body/reduce_sum | solution.py:55
  765.3 11.2 %multiply_reduce_fusion.6 = f32[32,32]{1,0:T(8,128)S(1)} fusion(f32[]{:T(128)} %bitcast.276, f32[]{:T(128)} %bitcast.277, f32[]{:T(128)} %bitcast.278, f32[]{:T(128)} %bitcast.279, bf16[32,128,128]{2,1,0:T(8,128)(2,1)S(1)} %get-tuple-element.591, s32[]{:T(128)S(6)} %select_n.395, s32[]{:T(128)S(6)} %select_n.397, f32[32,32,32]{2,1,0:T(8,128)S(1)} %fusion.133, ...), kind=kLoop, calls=%fused_computation.24.clone.1 | loop fusion | flops 1408000 | bytes 271432 | tf_op jit(solution)/shard_map/while/body/reduce_sum | solution.py:55
  776.6 11.1 %multiply_reduce_fusion.7 = f32[32,32]{1,0:T(8,128)S(1)} fusion(f32[]{:T(128)} %bitcast.281, f32[]{:T(128)} %bitcast.282, f32[]{:T(128)} %bitcast.283, f32[]{:T(128)} %bitcast.284, bf16[32,128,128]{2,1,0:T(8,128)(2,1)S(1)} %get-tuple-element.591, s32[]{:T(128)S(6)} %select_n.395, s32[]{:T(128)S(6)} %select_n.397, f32[32,32,32]{2,1,0:T(8,128)S(1)} %fusion.133, ...), kind=kLoop, calls=%fused_computation.25.clone.1 | loop fusion | flops 1408000 | bytes 271432 | tf_op jit(solution)/shard_map/while/body/reduce_sum | solution.py:55
  (271 shorter events, 478.4 us)
Async XLA Ops:
  0.6 19.3 %copy-start = (bf16[32,128,128]{2,1,0:T(8,128)(2,1)S(1)}, bf16[32,128,128]{2,1,0:T(8,128)(2,1)}, u32[]{:S(2)}) copy-start(bf16[32,128,128]{2,1,0:T(8,128)(2,1)} %param.13) | copy-start | bytes 3145732
  1.5 18.4 %collective-permute-start = (bf16[1,128,128]{2,1,0:T(8,128)(2,1)S(1)}, bf16[1,128,128]{2,1,0:T(8,128)(2,1)S(1)}, u32[]{:S(2)}, u32[]{:S(2)}) collective-permute-start(bf16[1,128,128]{2,1,0:T(8,128)(2,1)S(1)} %get-tuple-element.405), channel_id=1, source_target_pairs={{0,8},{8,16},{16,24},{1,9},{9,17},{17,25},{2,10},{10,18},{18,26},{... | collective-permute-start | bytes 98312 | tf_op jit(solution)/shard_map/ppermute | solution.py:16
  5.0 15.2 %collective-permute-start.1 = (bf16[1,128,128]{2,1,0:T(8,128)(2,1)S(1)}, bf16[1,128,128]{2,1,0:T(8,128)(2,1)S(1)}, u32[]{:S(2)}, u32[]{:S(2)}) collective-permute-start(bf16[1,128,128]{2,1,0:T(8,128)(2,1)S(1)} %get-tuple-element.404), channel_id=1, source_target_pairs={{8,0},{16,8},{24,16},{9,1},{17,9},{25,17},{10,2},{18,10},{26,18},{... | collective-permute-start | bytes 98312 | tf_op jit(solution)/shard_map/ppermute | solution.py:17
  23.7 18.3 %collective-permute-start.3 = (bf16[34,128,1]{1,0,2:T(8,128)(2,1)S(1)}, bf16[34,128,1]{1,0,2:T(8,128)(2,1)S(1)}, u32[]{:S(2)}, u32[]{:S(2)}) collective-permute-start(bf16[34,128,1]{1,0,2:T(8,128)(2,1)S(1)} %copy.42), channel_id=1, source_target_pairs={{2,0},{4,2},{6,4},{3,1},{5,3},{7,5},{10,8},{12,10},{14,12},{11,9},... | collective-permute-start | bytes 26120 | tf_op jit(solution)/shard_map/ppermute | solution.py:17
  27.9 15.6 %collective-permute-start.2 = (bf16[34,128,1]{1,0,2:T(8,128)(2,1)S(1)}, bf16[34,128,1]{1,0,2:T(8,128)(2,1)S(1)}, u32[]{:S(2)}, u32[]{:S(2)}) collective-permute-start(bf16[34,128,1]{1,0,2:T(8,128)(2,1)S(1)} %copy.41), channel_id=1, source_target_pairs={{0,2},{2,4},{4,6},{1,3},{3,5},{5,7},{8,10},{10,12},{12,14},{9,11},... | collective-permute-start | bytes 26120 | tf_op jit(solution)/shard_map/ppermute | solution.py:16
  44.9 8.0 copy-start.1
  44.9 8.0 copy-start.2
  46.3 6.6 collective-permute-start.5
  47.6 5.3 collective-permute-start.4
  58.8 16.3 %copy-start.5 = (f32[4,3]{1,0:T(4,128)S(1)}, f32[4,3]{1,0:T(4,128)}, u32[]{:S(2)}) copy-start(f32[4,3]{1,0:T(4,128)} %param.19) | copy-start | bytes 148
  58.9 16.3 %copy-start.6 = (f32[4]{0:T(128)S(1)}, f32[4]{0:T(128)}, u32[]{:S(2)}) copy-start(f32[4]{0:T(128)} %param.18) | copy-start | bytes 52
  58.9 16.3 %copy-start.7 = (f32[4]{0:T(128)S(1)}, f32[4]{0:T(128)}, u32[]{:S(2)}) copy-start(f32[4]{0:T(128)} %param.16) | copy-start | bytes 52
  58.9 16.3 %copy-start.8 = (f32[4]{0:T(128)S(1)}, f32[4]{0:T(128)}, u32[]{:S(2)}) copy-start(f32[4]{0:T(128)} %param.17) | copy-start | bytes 52
  60.2 15.0 %collective-permute-start.7 = (bf16[2,32,32,32]{3,2,1,0:T(8,128)(2,1)}, bf16[2,32,32,32]{3,2,1,0:T(8,128)(2,1)S(1)}, u32[]{:S(2)}, u32[]{:S(2)}) collective-permute-start(bf16[2,32,32,32]{3,2,1,0:T(8,128)(2,1)} %maximum_select_fusion), channel_id=1, source_target_pairs={{0,8},{8,0},{16,24},{24,16},{1,9},{9,1},{17,25},{25,17},{2,10},{10... | collective-permute-start | bytes 393224 | tf_op jit(solution)/shard_map/ppermute | solution.py:29
  62.8 12.3 %collective-permute-start.6 = (bf16[32,32]{0,1:T(8,128)(2,1)S(1)}, bf16[32,32]{0,1:T(8,128)(2,1)S(1)}, u32[]{:S(2)}, u32[]{:S(2)}) collective-permute-start(bf16[32,32]{0,1:T(8,128)(2,1)S(1)} %get-tuple-element.415), channel_id=1, source_target_pairs={{0,8},{8,0},{16,24},{24,16},{1,9},{9,1},{17,25},{25,17},{2,10},{10... | collective-permute-start | bytes 6152 | tf_op jit(solution)/shard_map/ppermute | solution.py:29
  62.9 737.7 %collective-permute-start.9 = (bf16[32,32]{0,1:T(8,128)(2,1)}, bf16[32,32]{0,1:T(8,128)(2,1)}, u32[]{:S(2)}, u32[]{:S(2)}) collective-permute-start(bf16[32,32]{0,1:T(8,128)(2,1)} %get-tuple-element.414), channel_id=1, source_target_pairs={{0,16},{16,0},{8,24},{24,8},{1,17},{17,1},{9,25},{25,9},{2,18},{18... | collective-permute-start | bytes 6152 | tf_op jit(solution)/shard_map/ppermute | solution.py:29
  71.8 728.7 %collective-permute-start.10 = (bf16[2,32,32,32]{3,2,1,0:T(8,128)(2,1)}, bf16[2,32,32,32]{3,2,1,0:T(8,128)(2,1)S(1)}, u32[]{:S(2)}, u32[]{:S(2)}) collective-permute-start(bf16[2,32,32,32]{3,2,1,0:T(8,128)(2,1)} %maximum_select_fusion.1), channel_id=1, source_target_pairs={{0,16},{16,0},{8,24},{24,8},{1,17},{17,1},{9,25},{25,9},{2,18},{18... | collective-permute-start | bytes 393224 | tf_op jit(solution)/shard_map/ppermute | solution.py:29
  75.9 725.0 %collective-permute-start.8 = (f32[4,32,32]{2,1,0:T(8,128)}, f32[4,32,32]{2,1,0:T(8,128)S(1)}, u32[]{:S(2)}, u32[]{:S(2)}) collective-permute-start(f32[4,32,32]{2,1,0:T(8,128)} %get-tuple-element.602), channel_id=1, source_target_pairs={{0,8},{8,0},{16,24},{24,16},{1,9},{9,1},{17,25},{25,17},{2,10},{10... | collective-permute-start | bytes 49160 | tf_op jit(solution)/shard_map/ppermute | solution.py:29
  800.8 5.2 collective-permute-start.11
  807.9 5.0 collective-permute-start.12
  813.1 5.2 collective-permute-start.13
where the time goes:
time: 828 us; the launch traced here: 820 us
  other arithmetic  595 us (72%)
  local copies, waits for them, and re-layouts  84.7 us (10%)
  starting transfers between devices  70.3 us (8%)
  loops' own time  36.4 us (4%)
  waiting for transfers between devices  16 us (2%)
  between operations  11.6 us (1%)
    reduce_sum x42, other arithmetic, render_cells(): parts = [jnp.sum(weight * emits[chan], axis=0) for chan in range(3)]  468 us
    another operation x14, other arithmetic, render_cells(): running = jnp.cumsum(tau, axis=0)  112 us
    ppermute x8, starting transfers between devices, from_partner(): return lax.ppermute(block, axis, route)  53.4 us
    another operation x1, loops' own time, local(): image = lax.fori_loop(0, count - handed[myself], paint, image)  36.1 us
    dynamic_update_slice x14, local copies, waits for them, and re-layouts, paint(): return lax.dynamic_update_slice(image, piece, (anchor, row, col))  21.2 us
  transfers between devices with their start and end apart: 14, of which 4 were waited for; matrix products, arithmetic and copies ran while one was open for 81% of the time, Pallas kernels for 0%

commit v1 on v0

v1 whole, which is shorter than its diff:
```python
import functools
import math

import jax
import jax.numpy as jnp
from jax import lax
from jax.experimental import pallas as pl
from jax.experimental.pallas import tpu as pltpu
from jax.sharding import PartitionSpec as P

OPTICAL = 3.0
MESH = pl.DeviceIdType.MESH
SUB = 8
PACK = 16
LANES = 128
F32 = jnp.float32
BF16 = jnp.bfloat16
LOG2E = math.log2(math.e)


def iota(shape, dim):
    return lax.broadcasted_iota(jnp.int32, shape, dim)


def expand(small, rows, cols):
    high, wide = small.shape
    down = (iota((rows, high), 0) // (rows // high) == iota((rows, high), 1)).astype(F32).astype(BF16)
    along = (iota((wide, cols), 1) // (cols // wide) == iota((wide, cols), 0)).astype(F32).astype(BF16)
    tall = jnp.dot(down, small.astype(F32).astype(BF16), preferred_element_type=F32)
    return jnp.dot(tall.astype(BF16), along, preferred_element_type=F32)


def kernel(
    counts, step_len,
    field, live, order, centers, widths, heights, colours,
    colour_out, logt_out,
    fb, vf, zlo, zhi, xlo, xhi, face, flo, fhi, gy, factor, flag, tiles_out, tiles_in,
    field_sem, halo_send, halo_recv, tile_send, tile_recv,
):
    ndepth, nimx, nimy = counts
    me = lax.axis_index("depth")
    mx = lax.axis_index("imx")
    my = lax.axis_index("imy")
    zdev, xdev, ydev = fb.shape
    rows_out = xdev // ndepth
    nb = centers.shape[0]
    rows_blk = min(PACK, rows_out)

    load = pltpu.make_async_copy(field, fb, field_sem)
    load.start()

    barrier = pltpu.get_barrier_semaphore()
    for step in range(1, ndepth):
        pl.semaphore_signal(barrier, inc=1, device_id={"depth": lax.rem(me + step, ndepth)}, device_id_type=MESH)
    for axis, pos, count in (("imx", mx, nimx), ("imy", my, nimy)):
        @pl.when(pos > 0)
        def _():
            pl.semaphore_signal(barrier, inc=1, device_id={axis: pos - 1}, device_id_type=MESH)

        @pl.when(pos < count - 1)
        def _():
            pl.semaphore_signal(barrier, inc=1, device_id={axis: pos + 1}, device_id_type=MESH)

    back = expand(order[...], xdev, ydev)
    flag[...] = back
    factor[...] = (2.0 * back - 1.0) * expand(live[0], xdev, ydev) * (step_len * LOG2E)

    for pos, count, low, high in ((me, ndepth, zlo, zhi), (mx, nimx, flo, fhi), (my, nimy, xlo, xhi)):
        @pl.when(pos == 0)
        def _():
            low[...] = jnp.zeros_like(low)

        @pl.when(pos == count - 1)
        def _():
            high[...] = jnp.zeros_like(high)

    peers = ndepth - 1
    for pos, count in ((mx, nimx), (my, nimy)):
        peers = peers + (pos + count - 1) // count + (2 * count - 2 - pos) // count
    pl.semaphore_wait(barrier, peers)
    load.wait()

    def links(axis, pos, count, down_src, up_src, low, high, at):
        to_low = pltpu.make_async_remote_copy(
            src_ref=down_src, dst_ref=high, send_sem=halo_send.at[at], recv_sem=halo_recv.at[at],
            device_id={axis: lax.rem(pos + count - 1, count)}, device_id_type=MESH)
        to_high = pltpu.make_async_remote_copy(
            src_ref=up_src, dst_ref=low, send_sem=halo_send.at[at + 1], recv_sem=halo_recv.at[at + 1],
            device_id={axis: lax.rem(pos + 1, count)}, device_id_type=MESH)
        return pos, count, to_low, to_high

    def start(link):
        pos, count, to_low, to_high = link

        @pl.when(pos > 0)
        def _():
            to_low.start()

        @pl.when(pos < count - 1)
        def _():
            to_high.start()

    def finish(link):
        pos, count, to_low, to_high = link

        @pl.when(pos > 0)
        def _():
            to_low.wait_send()
            to_high.wait_recv()

        @pl.when(pos < count - 1)
        def _():
            to_high.wait_send()
            to_low.wait_recv()

    zlink = links("depth", me, ndepth, fb.at[0], fb.at[zdev - 1], zlo, zhi, 0)
    xlink = links("imy", my, nimy, fb.at[:, pl.ds(0, PACK)], fb.at[:, pl.ds(xdev - PACK, PACK)], xlo, xhi, 2)
    ylink = links("imx", mx, nimx, face, face, flo, fhi, 4)
    start(zlink)
    start(xlink)

    k_at, l_at = iota((ydev, LANES), 0), iota((ydev, LANES), 1)
    pick = ((k_at == 0) & (l_at < zdev)) | ((k_at == ydev - 1) & (l_at >= zdev) & (l_at < 2 * zdev))
    pick = pick.astype(F32).astype(BF16)
    lane = iota((xdev, LANES), 1)

    def pack(z, acc):
        ends = jnp.dot(fb[z], pick, preferred_element_type=F32)
        return jnp.where((lane == z) | (lane == z + zdev), ends, acc)

    packed = lax.fori_loop(0, zdev, pack, jnp.zeros((xdev, LANES), F32), unroll=4)
    face[...] = packed.astype(BF16)
    start(ylink)

    def widen(z, carry):
        vf[z + 1, SUB:SUB + xdev] = fb[z].astype(F32)
        return carry

    lax.fori_loop(0, zdev, widen, 0, unroll=4)

    finish(zlink)
    vf[0, SUB:SUB + xdev] = zlo[...].astype(F32)
    vf[zdev + 1, SUB:SUB + xdev] = zhi[...].astype(F32)
    finish(xlink)

    def widen_rows(z, carry):
        vf[z + 1, 0:SUB] = xlo[z].astype(F32)[PACK - SUB:]
        vf[z + 1, SUB + xdev:] = xhi[z].astype(F32)[:SUB]
        return carry

    lax.fori_loop(0, zdev, widen_rows, 0, unroll=4)
    finish(ylink)

    edges = jnp.where(lane < zdev, fhi[...].astype(F32), flo[...].astype(F32))
    k_at, l_at = iota((ydev + LANES, ydev), 0), iota((ydev + LANES, ydev), 1)
    plus = (k_at == l_at + 1) & (k_at < ydev) | (k_at >= ydev) & (k_at < ydev + zdev) & (l_at == ydev - 1)
    minus = (k_at == l_at - 1) | (k_at >= ydev + zdev) & (k_at < ydev + 2 * zdev) & (l_at == 0)
    slope = (plus.astype(F32) - minus.astype(F32)).astype(BF16)

    def across(z, carry):
        side = jnp.where((lane == z) | (lane == z + zdev), edges, 0.0).astype(BF16)
        gy[z] = jnp.dot(jnp.concatenate([fb[z], side], axis=1), slope, preferred_element_type=F32)
        return carry

    lax.fori_loop(0, zdev, across, 0, unroll=4)

    cen = [centers[j] for j in range(nb)]
    hei = [heights[j] for j in range(nb)]
    cur = []
    for j in range(nb):
        wid = jnp.full((rows_blk, ydev), widths[j], F32)
        cur.append((-0.5 * LOG2E) / (wid * wid))

    def block(row):
        here = pl.ds(pl.multiple_of(row, SUB), rows_blk)
        body = pl.ds(pl.multiple_of(row + SUB, SUB), rows_blk)
        above = pl.ds(row + SUB - 1, rows_blk)
        below = pl.ds(row + SUB + 1, rows_blk)
        fac = factor[here]

        def sample(z, carry):
            prev, val, depth, gone, sums = carry
            after = vf[z + 2, body]
            dz = after - prev
            dx = vf[z + 1, below] - vf[z + 1, above]
            dy = gy[z, here]
            facing = (0.7 * 0.64) * dz + (0.7 * 0.48) * dx + (0.7 * 0.6) * dy
            shade = 0.3 + jnp.abs(facing) * lax.rsqrt(dz * dz + dx * dx + dy * dy + 4.0)
            shade = shade.astype(BF16).astype(F32)
            bumps = []
            sigma = None
            for j in range(nb):
                off = val - cen[j]
                bump = jnp.exp2(off * cur[j] * off)
                bumps.append(bump)
                sigma = hei[j] * bump if sigma is None else sigma + hei[j] * bump
            depth = depth + sigma * fac
            now = jnp.exp2(depth)
            weight = (now - gone) * shade
            sums = tuple(acc + weight * bump for acc, bump in zip(sums, bumps))
            return val, after, depth, now, sums

        zero = jnp.zeros((rows_blk, ydev), F32)
        init = (vf[0, body], vf[1, body], zero, zero + 1.0, (zero,) * nb)
        _, _, depth, _, sums = lax.fori_loop(0, zdev, sample, init, unroll=4)
        mark = flag[here] > 0.5
        scale = jnp.where(mark, jnp.exp2(-depth), -1.0)
        logt = jnp.where(mark, -depth, depth) * (1.0 / LOG2E)
        chans = []
        for chan in range(3):
            total = None
            for j in range(nb):
                term = colours[j, chan] * sums[j]
                total = term if total is None else total + term
            chans.append(total * scale)
        return chans + [logt]

    def tile(owner, dest, slot):
        def one(i, carry):
            local = pl.multiple_of(i * rows_blk, SUB)
            values = block(owner * rows_out + local)
            for chan, value in enumerate(values):
                dest[slot, chan, pl.ds(local, rows_blk)] = value
            return carry

        lax.fori_loop(0, rows_out // rows_blk, one, 0)

    def send_of(owner):
        return pltpu.make_async_remote_copy(
            src_ref=tiles_out.at[owner], dst_ref=tiles_in.at[me], send_sem=tile_send.at[owner],
            recv_sem=tile_recv.at[me], device_id={"depth": owner}, device_id_type=MESH)

    def other(step, carry):
        owner = lax.rem(me + step, ndepth)
        tile(owner, tiles_out, owner)
        send_of(owner).start()
        return carry

    lax.fori_loop(1, ndepth, other, 0)
    tile(me, tiles_in, me)

    for step in range(1, ndepth):
        owner = lax.rem(me + step, ndepth)
        pltpu.make_async_remote_copy(
            src_ref=tiles_out.at[owner], dst_ref=tiles_in.at[owner], send_sem=tile_send.at[owner],
            recv_sem=tile_recv.at[owner], device_id={"depth": owner}, device_id_type=MESH).wait()

    mark = flag[pl.ds(pl.multiple_of(me * rows_out, SUB), rows_out)] > 0.5
    zero = jnp.zeros((rows_out, ydev), F32)
    done, through, total = [zero] * 3, zero + 1.0, zero
    for slab in range(ndepth):
        logt = tiles_in[slab, 3]
        clear = jnp.exp(logt)
        keep = jnp.where(mark, clear, 1.0)
        ahead = jnp.where(mark, 1.0, through)
        done = [keep * done[chan] + ahead * tiles_in[slab, chan] for chan in range(3)]
        through = through * clear
        total = total + logt
    for chan in range(3):
        colour_out[chan] = done[chan]
    logt_out[...] = total


def local(field, brick_live, order, centers, widths, heights, colours):
    counts = tuple(lax.axis_size(axis) for axis in ("depth", "imx", "imy"))
    zdev, xdev, ydev = field.shape
    ndepth = counts[0]
    rows_out = xdev // ndepth
    step_len = OPTICAL / (zdev * ndepth)
    vmem = pl.BlockSpec(memory_space=pltpu.VMEM)
    smem = pl.BlockSpec(memory_space=pltpu.SMEM)
    dma = pltpu.SemaphoreType.DMA
    return pl.pallas_call(
        functools.partial(kernel, counts, step_len),
        out_shape=(
            jax.ShapeDtypeStruct((3, rows_out, ydev), F32),
            jax.ShapeDtypeStruct((rows_out, ydev), F32),
        ),
        in_specs=[pl.BlockSpec(memory_space=pl.ANY), vmem, vmem, smem, smem, smem, smem],
        out_specs=(vmem, vmem),
        scratch_shapes=[
            pltpu.VMEM((zdev, xdev, ydev), BF16),
            pltpu.VMEM((zdev + 2, xdev + 2 * SUB, ydev), F32),
            pltpu.VMEM((xdev, ydev), BF16),
            pltpu.VMEM((xdev, ydev), BF16),
            pltpu.VMEM((zdev, PACK, ydev), BF16),
            pltpu.VMEM((zdev, PACK, ydev), BF16),
            pltpu.VMEM((xdev, LANES), BF16),
            pltpu.VMEM((xdev, LANES), BF16),
            pltpu.VMEM((xdev, LANES), BF16),
            pltpu.VMEM((zdev, xdev, ydev), F32),
            pltpu.VMEM((xdev, ydev), F32),
            pltpu.VMEM((xdev, ydev), F32),
            pltpu.VMEM((ndepth, 4, rows_out, ydev), F32),
            pltpu.VMEM((ndepth, 4, rows_out, ydev), F32),
            dma,
            dma((6,)),
            dma((6,)),
            dma((ndepth,)),
            dma((ndepth,)),
        ],
        compiler_params=pltpu.CompilerParams(collective_id=0, has_side_effects=True),
    )(field, brick_live, order, centers, widths, heights, colours)


def solution(mesh):
    return jax.shard_map(
        local,
        mesh=mesh,
        in_specs=(
            P("depth", "imy", "imx"),
            P("depth", "imy", "imx"),
            P("imy", "imx"),
            P(),
            P(),
            P(),
            P(),
        ),
        out_specs=(P(None, ("imy", "depth"), "imx"), P(("imy", "depth"), "imx")),
        check_vma=False,
    )
```

time: 828 us -> 23.2 us (0.03)
  the two profiles are of different devices: /device:TPU:18 before, /device:TPU:0 now
where the time goes in v1:
time: 23.2 us; the launch traced here: 23 us
  Pallas kernels  20.3 us (88%)
  local copies, waits for them, and re-layouts  2.04 us (9%)
  between operations  0.65 us (3%)
    pallas_call x1, Pallas kernels, local(): pl.pallas_call(functools.partial(kernel, counts, step_len), out_shape=(ja...  20.3 us
    unnamed x4, local copies, waits for them, and re-layouts  2.04 us

profile of v1, /device:TPU:0, one launch (start us, length us, event | category | flops | bytes accessed | tf_op | source)
XLA Modules:
  0.0 23.0 jit_solution(15680711849902073560)
XLA Ops:
  0.6 20.3 %shard_map.86 = (f32[3,32,128]{2,1,0:T(8,128)}, f32[32,128]{1,0:T(8,128)}) custom-call(bf16[32,128,128]{2,1,0:T(8,128)(2,1)} %field.1, s32[1,4,4]{2,1,0:T(4,128)} %live.1, s32[16,16]{1,0:T(8,128)} %order.1, f32[4]{0:T(128)} %centers.1, f32[4]{0:T(128)} %widths.1, f32[4]{0:T(128)} %heights.1, f32[4,3]{1,0:T(4,128)} %colours.1), custom_call_target="tpu_custom_call" | custom-call | tf_op jit(solution)/shard_map/pallas_call | solution.py:273
  21.0 0.0 copy-start
  21.0 1.4 %copy.11 = f32[3,32,128]{2,1,0:T(8,128)} copy(f32[3,32,128]{2,1,0:T(8,128)} %get-tuple-element.4) | data formatting | bytes 98304
  22.4 0.0 copy-done
  22.4 0.6 %copy.12 = f32[32,128]{1,0:T(8,128)} copy(f32[32,128]{1,0:T(8,128)S(1)} %copy-done) | data formatting | bytes 32768
Async XLA Ops:
  21.0 1.4 %copy-start = (f32[32,128]{1,0:T(8,128)S(1)}, f32[32,128]{1,0:T(8,128)}, u32[]{:S(2)}) copy-start(f32[32,128]{1,0:T(8,128)} %get-tuple-element.5) | copy-start | bytes 49156

commit v2 on v1

--- a/solution.py
+++ b/solution.py
@@ -12,7 +12,6 @@
 MESH = pl.DeviceIdType.MESH
 SUB = 8
 PACK = 16
-LANES = 128
 F32 = jnp.float32
 BF16 = jnp.bfloat16
 LOG2E = math.log2(math.e)
@@ -32,10 +31,11 @@
 
 def kernel(
     counts, step_len,
-    field, live, order, centers, widths, heights, colours,
+    field, live_in, order_in, centers_in, widths_in, heights_in, colours_in,
     colour_out, logt_out,
-    fb, vf, zlo, zhi, xlo, xhi, face, flo, fhi, gy, factor, flag, tiles_out, tiles_in,
-    field_sem, halo_send, halo_recv, tile_send, tile_recv,
+    fb, live, order, centers, widths, heights, colours,
+    vf, zlo, zhi, xlo, xhi, face, flo, fhi, weights, lobes, scales, flag, logs, logs_in, tiles_out, tiles_in, edges,
+    load_sem, halo_send, halo_recv, log_send, log_recv, tile_send, tile_recv,
 ):
     ndepth, nimx, nimy = counts
     me = lax.axis_index("depth")
@@ -46,8 +46,11 @@
     nb = centers.shape[0]
     rows_blk = min(PACK, rows_out)
 
-    load = pltpu.make_async_copy(field, fb, field_sem)
-    load.start()
+    pairs = ((field, fb), (order_in, order), (live_in, live), (centers_in, centers),
+             (widths_in, widths), (heights_in, heights), (colours_in, colours))
+    loads = [pltpu.make_async_copy(src, dst, load_sem.at[at]) for at, (src, dst) in enumerate(pairs)]
+    for load in loads:
+        load.start()
 
     barrier = pltpu.get_barrier_semaphore()
     for step in range(1, ndepth):
@@ -61,10 +64,6 @@
         def _():
             pl.semaphore_signal(barrier, inc=1, device_id={axis: pos + 1}, device_id_type=MESH)
 
-    back = expand(order[...], xdev, ydev)
-    flag[...] = back
-    factor[...] = (2.0 * back - 1.0) * expand(live[0], xdev, ydev) * (step_len * LOG2E)
-
     for pos, count, low, high in ((me, ndepth, zlo, zhi), (mx, nimx, flo, fhi), (my, nimy, xlo, xhi)):
         @pl.when(pos == 0)
         def _():
@@ -78,7 +77,7 @@
     for pos, count in ((mx, nimx), (my, nimy)):
         peers = peers + (pos + count - 1) // count + (2 * count - 2 - pos) // count
     pl.semaphore_wait(barrier, peers)
-    load.wait()
+    loads[0].wait()
 
     def links(axis, pos, count, down_src, up_src, low, high, at):
         to_low = pltpu.make_async_remote_copy(
@@ -119,51 +118,22 @@
     start(zlink)
     start(xlink)
 
-    k_at, l_at = iota((ydev, LANES), 0), iota((ydev, LANES), 1)
-    pick = ((k_at == 0) & (l_at < zdev)) | ((k_at == ydev - 1) & (l_at >= zdev) & (l_at < 2 * zdev))
-    pick = pick.astype(F32).astype(BF16)
-    lane = iota((xdev, LANES), 1)
-
-    def pack(z, acc):
-        ends = jnp.dot(fb[z], pick, preferred_element_type=F32)
-        return jnp.where((lane == z) | (lane == z + zdev), ends, acc)
-
-    packed = lax.fori_loop(0, zdev, pack, jnp.zeros((xdev, LANES), F32), unroll=4)
-    face[...] = packed.astype(BF16)
+    lane = iota((xdev, ydev), 1)
+
+    def widen(z, packed):
+        value = fb[z].astype(F32)
+        vf[z + 1, SUB:SUB + xdev] = value
+        return jnp.where(lane // 2 == z, pltpu.roll(value, 2 * z + 1, 1), packed)
+
+    face[...] = lax.fori_loop(0, zdev, widen, jnp.zeros((xdev, ydev), F32), unroll=4).astype(BF16)
     start(ylink)
 
-    def widen(z, carry):
-        vf[z + 1, SUB:SUB + xdev] = fb[z].astype(F32)
-        return carry
-
-    lax.fori_loop(0, zdev, widen, 0, unroll=4)
-
-    finish(zlink)
-    vf[0, SUB:SUB + xdev] = zlo[...].astype(F32)
-    vf[zdev + 1, SUB:SUB + xdev] = zhi[...].astype(F32)
-    finish(xlink)
-
-    def widen_rows(z, carry):
-        vf[z + 1, 0:SUB] = xlo[z].astype(F32)[PACK - SUB:]
-        vf[z + 1, SUB + xdev:] = xhi[z].astype(F32)[:SUB]
-        return carry
-
-    lax.fori_loop(0, zdev, widen_rows, 0, unroll=4)
-    finish(ylink)
-
-    edges = jnp.where(lane < zdev, fhi[...].astype(F32), flo[...].astype(F32))
-    k_at, l_at = iota((ydev + LANES, ydev), 0), iota((ydev + LANES, ydev), 1)
-    plus = (k_at == l_at + 1) & (k_at < ydev) | (k_at >= ydev) & (k_at < ydev + zdev) & (l_at == ydev - 1)
-    minus = (k_at == l_at - 1) | (k_at >= ydev + zdev) & (k_at < ydev + 2 * zdev) & (l_at == 0)
-    slope = (plus.astype(F32) - minus.astype(F32)).astype(BF16)
-
-    def across(z, carry):
-        side = jnp.where((lane == z) | (lane == z + zdev), edges, 0.0).astype(BF16)
-        gy[z] = jnp.dot(jnp.concatenate([fb[z], side], axis=1), slope, preferred_element_type=F32)
-        return carry
-
-    lax.fori_loop(0, zdev, across, 0, unroll=4)
-
+    for load in loads[1:]:
+        load.wait()
+    back = expand(order[...], xdev, ydev)
+    factor = (2.0 * back - 1.0) * expand(live[0], xdev, ydev) * (step_len * LOG2E)
+    flag[...] = back
+    scales[...] = factor
     cen = [centers[j] for j in range(nb)]
     hei = [heights[j] for j in range(nb)]
     cur = []
@@ -171,41 +141,84 @@
         wid = jnp.full((rows_blk, ydev), widths[j], F32)
         cur.append((-0.5 * LOG2E) / (wid * wid))
 
+    def absorb(i, carry):
+        row = i * rows_blk
+        here = pl.ds(pl.multiple_of(row, SUB), rows_blk)
+        body = pl.ds(pl.multiple_of(row + SUB, SUB), rows_blk)
+        fac = scales[here]
+
+        def sample(z, carry):
+            depth, gone = carry
+            val = vf[z + 1, body]
+            sigma = None
+            for j in range(nb):
+                off = val - cen[j]
+                bump = jnp.exp2(off * cur[j] * off)
+                lobes[j, z, here] = bump
+                sigma = hei[j] * bump if sigma is None else sigma + hei[j] * bump
+            depth = depth + sigma * fac
+            now = jnp.exp2(depth)
+            weights[z, here] = now - gone
+            return depth, now
+
+        zero = jnp.zeros((rows_blk, ydev), F32)
+        depth, _ = lax.fori_loop(0, zdev, sample, (zero, zero + 1.0), unroll=4)
+        mark = flag[here] > 0.5
+        scales[here] = jnp.where(mark, jnp.exp2(-depth), -1.0)
+        logs[here] = jnp.where(mark, -depth, depth) * (1.0 / LOG2E)
+        return carry
+
+    lax.fori_loop(0, xdev // rows_blk, absorb, 0)
+
+    def log_copy(owner, source):
+        return pltpu.make_async_remote_copy(
+            src_ref=logs.at[pl.ds(pl.multiple_of(owner * rows_out, SUB), rows_out)], dst_ref=logs_in.at[source],
+            send_sem=log_send.at[owner], recv_sem=log_recv.at[source], device_id={"depth": owner}, device_id_type=MESH)
+
+    for step in range(1, ndepth):
+        log_copy(lax.rem(me + step, ndepth), me).start()
+    logs_in[me] = logs[pl.ds(pl.multiple_of(me * rows_out, SUB), rows_out)]
+    finish(zlink)
+    vf[0, SUB:SUB + xdev] = zlo[...].astype(F32)
+    vf[zdev + 1, SUB:SUB + xdev] = zhi[...].astype(F32)
+    finish(xlink)
+
+    def widen_rows(z, carry):
+        vf[z + 1, 0:SUB] = xlo[z].astype(F32)[PACK - SUB:]
+        vf[z + 1, SUB + xdev:] = xhi[z].astype(F32)[:SUB]
+        return carry
+
+    lax.fori_loop(0, zdev, widen_rows, 0, unroll=4)
+    finish(ylink)
+
+    fromleft = pltpu.roll(flo[...].astype(F32), 1, 1)
+    fromright = pltpu.roll(fhi[...].astype(F32), ydev - 1, 1)
+    edges[...] = pltpu.roll(jnp.where(lane % 2 == 0, fromright, fromleft), ydev - 1, 1)
+    spot = iota((rows_blk, ydev), 1)
+    first, last = spot == 0, spot == ydev - 1
+
     def block(row):
         here = pl.ds(pl.multiple_of(row, SUB), rows_blk)
         body = pl.ds(pl.multiple_of(row + SUB, SUB), rows_blk)
         above = pl.ds(row + SUB - 1, rows_blk)
         below = pl.ds(row + SUB + 1, rows_blk)
-        fac = factor[here]
 
         def sample(z, carry):
-            prev, val, depth, gone, sums = carry
+            prev, val, side, sums = carry
             after = vf[z + 2, body]
             dz = after - prev
             dx = vf[z + 1, below] - vf[z + 1, above]
-            dy = gy[z, here]
+            dy = jnp.where(last, side, pltpu.roll(val, ydev - 1, 1)) - jnp.where(first, side, pltpu.roll(val, 1, 1))
             facing = (0.7 * 0.64) * dz + (0.7 * 0.48) * dx + (0.7 * 0.6) * dy
             shade = 0.3 + jnp.abs(facing) * lax.rsqrt(dz * dz + dx * dx + dy * dy + 4.0)
-            shade = shade.astype(BF16).astype(F32)
-            bumps = []
-            sigma = None
-            for j in range(nb):
-                off = val - cen[j]
-                bump = jnp.exp2(off * cur[j] * off)
-                bumps.append(bump)
-                sigma = hei[j] * bump if sigma is None else sigma + hei[j] * bump
-            depth = depth + sigma * fac
-            now = jnp.exp2(depth)
-            weight = (now - gone) * shade
-            sums = tuple(acc + weight * bump for acc, bump in zip(sums, bumps))
-            return val, after, depth, now, sums
+            weight = weights[z, here] * shade.astype(BF16).astype(F32)
+            sums = tuple(acc + weight * lobes[j, z, here] for j, acc in enumerate(sums))
+            return val, after, pltpu.roll(side, ydev - 2, 1), sums
 
         zero = jnp.zeros((rows_blk, ydev), F32)
-        init = (vf[0, body], vf[1, body], zero, zero + 1.0, (zero,) * nb)
-        _, _, depth, _, sums = lax.fori_loop(0, zdev, sample, init, unroll=4)
-        mark = flag[here] > 0.5
-        scale = jnp.where(mark, jnp.exp2(-depth), -1.0)
-        logt = jnp.where(mark, -depth, depth) * (1.0 / LOG2E)
+        init = (vf[0, body], vf[1, body], edges[here], (zero,) * nb)
+        _, _, _, sums = lax.fori_loop(0, zdev, sample, init, unroll=4)
+        scale = scales[here]
         chans = []
         for chan in range(3):
             total = None
@@ -213,7 +226,7 @@
                 term = colours[j, chan] * sums[j]
                 total = term if total is None else total + term
             chans.append(total * scale)
-        return chans + [logt]
+        return chans
 
     def tile(owner, dest, slot):
         def one(i, carry):
@@ -244,12 +257,13 @@
         pltpu.make_async_remote_copy(
             src_ref=tiles_out.at[owner], dst_ref=tiles_in.at[owner], send_sem=tile_send.at[owner],
             recv_sem=tile_recv.at[owner], device_id={"depth": owner}, device_id_type=MESH).wait()
+        log_copy(owner, owner).wait()
 
     mark = flag[pl.ds(pl.multiple_of(me * rows_out, SUB), rows_out)] > 0.5
     zero = jnp.zeros((rows_out, ydev), F32)
     done, through, total = [zero] * 3, zero + 1.0, zero
     for slab in range(ndepth):
-        logt = tiles_in[slab, 3]
+        logt = logs_in[slab]
         clear = jnp.exp(logt)
         keep = jnp.where(mark, clear, 1.0)
         ahead = jnp.where(mark, 1.0, through)
@@ -268,34 +282,45 @@
     rows_out = xdev // ndepth
     step_len = OPTICAL / (zdev * ndepth)
     vmem = pl.BlockSpec(memory_space=pltpu.VMEM)
-    smem = pl.BlockSpec(memory_space=pltpu.SMEM)
     dma = pltpu.SemaphoreType.DMA
     return pl.pallas_call(
         functools.partial(kernel, counts, step_len),
         out_shape=(
-            jax.ShapeDtypeStruct((3, rows_out, ydev), F32),
-            jax.ShapeDtypeStruct((rows_out, ydev), F32),
+            pltpu.VMEM((3, rows_out, ydev), F32),
+            pltpu.VMEM((rows_out, ydev), F32),
         ),
-        in_specs=[pl.BlockSpec(memory_space=pl.ANY), vmem, vmem, smem, smem, smem, smem],
+        in_specs=[pl.BlockSpec(memory_space=pl.ANY)] * 7,
         out_specs=(vmem, vmem),
         scratch_shapes=[
             pltpu.VMEM((zdev, xdev, ydev), BF16),
+            pltpu.VMEM(brick_live.shape, jnp.int32),
+            pltpu.VMEM(order.shape, jnp.int32),
+            pltpu.SMEM(centers.shape, F32),
+            pltpu.SMEM(widths.shape, F32),
+            pltpu.SMEM(heights.shape, F32),
+            pltpu.SMEM(colours.shape, F32),
             pltpu.VMEM((zdev + 2, xdev + 2 * SUB, ydev), F32),
             pltpu.VMEM((xdev, ydev), BF16),
             pltpu.VMEM((xdev, ydev), BF16),
             pltpu.VMEM((zdev, PACK, ydev), BF16),
             pltpu.VMEM((zdev, PACK, ydev), BF16),
-            pltpu.VMEM((xdev, LANES), BF16),
-            pltpu.VMEM((xdev, LANES), BF16),
-            pltpu.VMEM((xdev, LANES), BF16),
+            pltpu.VMEM((xdev, ydev), BF16),
+            pltpu.VMEM((xdev, ydev), BF16),
+            pltpu.VMEM((xdev, ydev), BF16),
             pltpu.VMEM((zdev, xdev, ydev), F32),
+            pltpu.VMEM((centers.shape[0], zdev, xdev, ydev), F32),
             pltpu.VMEM((xdev, ydev), F32),
             pltpu.VMEM((xdev, ydev), F32),
-            pltpu.VMEM((ndepth, 4, rows_out, ydev), F32),
-            pltpu.VMEM((ndepth, 4, rows_out, ydev), F32),
-            dma,
+            pltpu.VMEM((xdev, ydev), F32),
+            pltpu.VMEM((ndepth, rows_out, ydev), F32),
+            pltpu.VMEM((ndepth, 3, rows_out, ydev), F32),
+            pltpu.VMEM((ndepth, 3, rows_out, ydev), F32),
+            pltpu.VMEM((xdev, ydev), F32),
+            dma((7,)),
             dma((6,)),
             dma((6,)),
+            dma((ndepth,)),
+            dma((ndepth,)),
             dma((ndepth,)),
             dma((ndepth,)),
         ],

time: 23.2 us -> 29.3 us (1.26)
  Pallas kernels: 20.3 us -> 27.3 us
  local copies, waits for them, and re-layouts: 2.04 us -> 1.23 us
    pallas_call x1, Pallas kernels: 20.3 us -> 27.3 us  [local(): pl.pallas_call(functools.partial(kernel, counts, step_len), out_shape=(pl...]
    unnamed x4 -> x2, local copies, waits for them, and re-layouts: 2.04 us -> 1.23 us
where the time goes in v2:
time: 29.3 us; the launch traced here: 29.2 us
  Pallas kernels  27.3 us (93%)
  local copies, waits for them, and re-layouts  1.23 us (4%)
  between operations  0.64 us (2%)
    pallas_call x1, Pallas kernels, local(): pl.pallas_call(functools.partial(kernel, counts, step_len), out_shape=(pl...  27.3 us
    unnamed x2, local copies, waits for them, and re-layouts  1.23 us

profile of v2, /device:TPU:0, one launch (start us, length us, event | category | flops | bytes accessed | tf_op | source)
XLA Modules:
  0.0 29.2 jit_solution(2521133711169074317)
XLA Ops:
  0.6 27.3 %shard_map.86 = (f32[3,32,128]{2,1,0:T(8,128)S(1)}, f32[32,128]{1,0:T(8,128)S(1)}) custom-call(bf16[32,128,128]{2,1,0:T(8,128)(2,1)} %field.1, s32[1,4,4]{2,1,0:T(4,128)} %live_in.1, s32[16,16]{1,0:T(8,128)} %order_in.1, f32[4]{0:T(128)} %centers_in.1, f32[4]{0:T(128)} %widths_in.1, f32[4]{0:T(128)} %heights_in.1, f32[4,3]{1,0:T(4,128)} %colours_in.1), custom_call_target="tpu_custom_call" | custom-call | tf_op jit(solution)/shard_map/pallas_call | solution.py:286
  27.9 0.6 %copy.11 = f32[3,32,128]{2,1,0:T(8,128)} copy(f32[3,32,128]{2,1,0:T(8,128)S(1)} %get-tuple-element.2) | data formatting | bytes 98304
  28.6 0.6 %copy.12 = f32[32,128]{1,0:T(8,128)} copy(f32[32,128]{1,0:T(8,128)S(1)} %get-tuple-element.3) | data formatting | bytes 32768

commit v3 on v2

--- a/solution.py
+++ b/solution.py
@@ -34,7 +34,7 @@
     field, live_in, order_in, centers_in, widths_in, heights_in, colours_in,
     colour_out, logt_out,
     fb, live, order, centers, widths, heights, colours,
-    vf, zlo, zhi, xlo, xhi, face, flo, fhi, weights, lobes, scales, flag, logs, logs_in, tiles_out, tiles_in, edges,
+    vf, zlo, zhi, xlo, xhi, face, flo, fhi, weights, lobes, scales, flag, logs, logs_in, tiles_out, tiles_in, gy,
     load_sem, halo_send, halo_recv, log_send, log_recv, tile_send, tile_recv,
 ):
     ndepth, nimx, nimy = counts
@@ -125,7 +125,7 @@
         vf[z + 1, SUB:SUB + xdev] = value
         return jnp.where(lane // 2 == z, pltpu.roll(value, 2 * z + 1, 1), packed)
 
-    face[...] = lax.fori_loop(0, zdev, widen, jnp.zeros((xdev, ydev), F32), unroll=4).astype(BF16)
+    face[...] = lax.fori_loop(0, zdev, widen, jnp.zeros((xdev, ydev), F32), unroll=8).astype(BF16)
     start(ylink)
 
     for load in loads[1:]:
@@ -162,7 +162,7 @@
             return depth, now
 
         zero = jnp.zeros((rows_blk, ydev), F32)
-        depth, _ = lax.fori_loop(0, zdev, sample, (zero, zero + 1.0), unroll=4)
+        depth, _ = lax.fori_loop(0, zdev, sample, (zero, zero + 1.0), unroll=8)
         mark = flag[here] > 0.5
         scales[here] = jnp.where(mark, jnp.exp2(-depth), -1.0)
         logs[here] = jnp.where(mark, -depth, depth) * (1.0 / LOG2E)
@@ -193,9 +193,19 @@
 
     fromleft = pltpu.roll(flo[...].astype(F32), 1, 1)
     fromright = pltpu.roll(fhi[...].astype(F32), ydev - 1, 1)
-    edges[...] = pltpu.roll(jnp.where(lane % 2 == 0, fromright, fromleft), ydev - 1, 1)
-    spot = iota((rows_blk, ydev), 1)
-    first, last = spot == 0, spot == ydev - 1
+    edges = jnp.where(lane % 2 == 0, fromright, fromleft)
+    k_at, l_at = iota((2 * ydev, ydev), 0), iota((2 * ydev, ydev), 1)
+    odd = k_at % 2 == 1
+    plus = (k_at < ydev) & (k_at == l_at + 1) | (k_at >= ydev) & (l_at == ydev - 1) & jnp.logical_not(odd)
+    minus = (k_at < ydev) & (k_at == l_at - 1) | (k_at >= ydev) & (l_at == 0) & odd
+    slope = (plus.astype(F32) - minus.astype(F32)).astype(BF16)
+
+    def across(z, carry):
+        side = jnp.where(lane // 2 == z, edges, 0.0).astype(BF16)
+        gy[z] = jnp.dot(jnp.concatenate([fb[z], side], axis=1), slope, preferred_element_type=F32)
+        return carry
+
+    lax.fori_loop(0, zdev, across, 0, unroll=16)
 
     def block(row):
         here = pl.ds(pl.multiple_of(row, SUB), rows_blk)
@@ -204,20 +214,20 @@
         below = pl.ds(row + SUB + 1, rows_blk)
 
         def sample(z, carry):
-            prev, val, side, sums = carry
+            prev, val, sums = carry
             after = vf[z + 2, body]
             dz = after - prev
             dx = vf[z + 1, below] - vf[z + 1, above]
-            dy = jnp.where(last, side, pltpu.roll(val, ydev - 1, 1)) - jnp.where(first, side, pltpu.roll(val, 1, 1))
+            dy = gy[z, here]
             facing = (0.7 * 0.64) * dz + (0.7 * 0.48) * dx + (0.7 * 0.6) * dy
             shade = 0.3 + jnp.abs(facing) * lax.rsqrt(dz * dz + dx * dx + dy * dy + 4.0)
             weight = weights[z, here] * shade.astype(BF16).astype(F32)
             sums = tuple(acc + weight * lobes[j, z, here] for j, acc in enumerate(sums))
-            return val, after, pltpu.roll(side, ydev - 2, 1), sums
+            return val, after, sums
 
         zero = jnp.zeros((rows_blk, ydev), F32)
-        init = (vf[0, body], vf[1, body], edges[here], (zero,) * nb)
-        _, _, _, sums = lax.fori_loop(0, zdev, sample, init, unroll=4)
+        init = (vf[0, body], vf[1, body], (zero,) * nb)
+        _, _, sums = lax.fori_loop(0, zdev, sample, init, unroll=8)
         scale = scales[here]
         chans = []
         for chan in range(3):
@@ -315,7 +325,7 @@
             pltpu.VMEM((ndepth, rows_out, ydev), F32),
             pltpu.VMEM((ndepth, 3, rows_out, ydev), F32),
             pltpu.VMEM((ndepth, 3, rows_out, ydev), F32),
-            pltpu.VMEM((xdev, ydev), F32),
+            pltpu.VMEM((zdev, xdev, ydev), F32),
             dma((7,)),
             dma((6,)),
             dma((6,)),

time: 29.3 us -> 17.7 us (0.60)
  Pallas kernels: 27.3 us -> 15.7 us
    pallas_call x1, Pallas kernels: 27.3 us -> 15.7 us  [local(): pl.pallas_call(functools.partial(kernel, counts, step_len), out_shape=(pl...]
where the time goes in v3:
time: 17.7 us; the launch traced here: 17.6 us
  Pallas kernels  15.7 us (89%)
  local copies, waits for them, and re-layouts  1.23 us (7%)
  between operations  0.64 us (4%)
    pallas_call x1, Pallas kernels, local(): pl.pallas_call(functools.partial(kernel, counts, step_len), out_shape=(pl...  15.7 us
    unnamed x2, local copies, waits for them, and re-layouts  1.23 us

profile of v3, /device:TPU:0, one launch (start us, length us, event | category | flops | bytes accessed | tf_op | source)
XLA Modules:
  0.0 17.6 jit_solution(4112124804864405001)
XLA Ops:
  0.6 15.7 %shard_map.86 = (f32[3,32,128]{2,1,0:T(8,128)S(1)}, f32[32,128]{1,0:T(8,128)S(1)}) custom-call(bf16[32,128,128]{2,1,0:T(8,128)(2,1)} %field.1, s32[1,4,4]{2,1,0:T(4,128)} %live_in.1, s32[16,16]{1,0:T(8,128)} %order_in.1, f32[4]{0:T(128)} %centers_in.1, f32[4]{0:T(128)} %widths_in.1, f32[4]{0:T(128)} %heights_in.1, f32[4,3]{1,0:T(4,128)} %colours_in.1), custom_call_target="tpu_custom_call" | custom-call | tf_op jit(solution)/shard_map/pallas_call | solution.py:296
  16.3 0.6 %copy.11 = f32[3,32,128]{2,1,0:T(8,128)} copy(f32[3,32,128]{2,1,0:T(8,128)S(1)} %get-tuple-element.2) | data formatting | bytes 98304
  17.0 0.6 %copy.12 = f32[32,128]{1,0:T(8,128)} copy(f32[32,128]{1,0:T(8,128)S(1)} %get-tuple-element.3) | data formatting | bytes 32768

commit v4 on v3

--- a/solution.py
+++ b/solution.py
@@ -14,6 +14,7 @@
 PACK = 16
 F32 = jnp.float32
 BF16 = jnp.bfloat16
+LEVELS = 32000.0
 LOG2E = math.log2(math.e)
 
 
@@ -34,8 +35,8 @@
     field, live_in, order_in, centers_in, widths_in, heights_in, colours_in,
     colour_out, logt_out,
     fb, live, order, centers, widths, heights, colours,
-    vf, zlo, zhi, xlo, xhi, face, flo, fhi, weights, lobes, scales, flag, logs, logs_in, tiles_out, tiles_in, gy,
-    load_sem, halo_send, halo_recv, log_send, log_recv, tile_send, tile_recv,
+    vf, zlo, zhi, xlo, xhi, face, flo, fhi, weights, lobes, scales, flag, logs, logs_in, tiles_out, tiles_in, gy, stage, peaks_out, peaks_in,
+    load_sem, halo_send, halo_recv, log_send, log_recv, tile_send, tile_recv, peak_send, peak_recv,
 ):
     ndepth, nimx, nimy = counts
     me = lax.axis_index("depth")
@@ -238,35 +239,52 @@
             chans.append(total * scale)
         return chans
 
-    def tile(owner, dest, slot):
+    def tile(owner):
         def one(i, carry):
             local = pl.multiple_of(i * rows_blk, SUB)
             values = block(owner * rows_out + local)
             for chan, value in enumerate(values):
-                dest[slot, chan, pl.ds(local, rows_blk)] = value
+                stage[chan, pl.ds(local, rows_blk)] = value
             return carry
 
         lax.fori_loop(0, rows_out // rows_blk, one, 0)
 
-    def send_of(owner):
-        return pltpu.make_async_remote_copy(
-            src_ref=tiles_out.at[owner], dst_ref=tiles_in.at[me], send_sem=tile_send.at[owner],
-            recv_sem=tile_recv.at[me], device_id={"depth": owner}, device_id_type=MESH)
+    def sends(owner, source):
+        place = {"depth": owner}
+        return (
+            pltpu.make_async_remote_copy(
+                src_ref=tiles_out.at[owner], dst_ref=tiles_in.at[source], send_sem=tile_send.at[owner],
+                recv_sem=tile_recv.at[source], device_id=place, device_id_type=MESH),
+            pltpu.make_async_remote_copy(
+                src_ref=peaks_out.at[owner], dst_ref=peaks_in.at[source], send_sem=peak_send.at[owner],
+                recv_sem=peak_recv.at[source], device_id=place, device_id_type=MESH),
+        )
+
+    tiles_in[me] = jnp.zeros((3, rows_out, ydev), jnp.int16)
+    peaks_in[me] = jnp.zeros((SUB, ydev), F32)
 
     def other(step, carry):
         owner = lax.rem(me + step, ndepth)
-        tile(owner, tiles_out, owner)
-        send_of(owner).start()
+        tile(owner)
+        line = iota((SUB, ydev), 0)
+        peaks = jnp.zeros((SUB, ydev), F32)
+        for chan in range(3):
+            value = stage[chan]
+            peak = jnp.maximum(jnp.max(value, axis=0, keepdims=True), 1e-30)
+            peaks = jnp.where(line == chan, peak * (1.0 / LEVELS), peaks)
+            tiles_out[owner, chan] = (value * (LEVELS / peak) + 0.5).astype(jnp.int32).astype(jnp.int16)
+        peaks_out[owner] = peaks
+        for copy in sends(owner, me):
+            copy.start()
         return carry
 
     lax.fori_loop(1, ndepth, other, 0)
-    tile(me, tiles_in, me)
+    tile(me)
 
     for step in range(1, ndepth):
         owner = lax.rem(me + step, ndepth)
-        pltpu.make_async_remote_copy(
-            src_ref=tiles_out.at[owner], dst_ref=tiles_in.at[owner], send_sem=tile_send.at[owner],
-            recv_sem=tile_recv.at[owner], device_id={"depth": owner}, device_id_type=MESH).wait()
+        for copy in sends(owner, owner):
+            copy.wait()
         log_copy(owner, owner).wait()
 
     mark = flag[pl.ds(pl.multiple_of(me * rows_out, SUB), rows_out)] > 0.5
@@ -277,7 +295,10 @@
         clear = jnp.exp(logt)
         keep = jnp.where(mark, clear, 1.0)
         ahead = jnp.where(mark, 1.0, through)
-        done = [keep * done[chan] + ahead * tiles_in[slab, chan] for chan in range(3)]
+        for chan in range(3):
+            value = tiles_in[slab, chan].astype(jnp.int32).astype(F32) * peaks_in[slab, chan:chan + 1]
+            value = jnp.where(me == slab, stage[chan], value)
+            done[chan] = keep * done[chan] + ahead * value
         through = through * clear
         total = total + logt
     for chan in range(3):
@@ -323,12 +344,17 @@
             pltpu.VMEM((xdev, ydev), F32),
             pltpu.VMEM((xdev, ydev), F32),
             pltpu.VMEM((ndepth, rows_out, ydev), F32),
-            pltpu.VMEM((ndepth, 3, rows_out, ydev), F32),
-            pltpu.VMEM((ndepth, 3, rows_out, ydev), F32),
+            pltpu.VMEM((ndepth, 3, rows_out, ydev), jnp.int16),
+            pltpu.VMEM((ndepth, 3, rows_out, ydev), jnp.int16),
             pltpu.VMEM((zdev, xdev, ydev), F32),
+            pltpu.VMEM((3, rows_out, ydev), F32),
+            pltpu.VMEM((ndepth, SUB, ydev), F32),
+            pltpu.VMEM((ndepth, SUB, ydev), F32),
             dma((7,)),
             dma((6,)),
             dma((6,)),
+            dma((ndepth,)),
+            dma((ndepth,)),
             dma((ndepth,)),
             dma((ndepth,)),
             dma((ndepth,)),

time: 17.7 us -> 16.8 us (0.949)
  Pallas kernels: 15.7 us -> 14.7 us
    pallas_call x1, Pallas kernels: 15.7 us -> 14.7 us  [local(): pl.pallas_call(functools.partial(kernel, counts, step_len), out_shape=(pl...]
where the time goes in v4:
time: 16.8 us; the launch traced here: 16.6 us
  Pallas kernels  14.7 us (88%)
  local copies, waits for them, and re-layouts  1.23 us (7%)
  between operations  0.64 us (4%)
    pallas_call x1, Pallas kernels, local(): pl.pallas_call(functools.partial(kernel, counts, step_len), out_shape=(pl...  14.7 us
    unnamed x2, local copies, waits for them, and re-layouts  1.23 us

profile of v4, /device:TPU:0, one launch (start us, length us, event | category | flops | bytes accessed | tf_op | source)
XLA Modules:
  0.0 16.6 jit_solution(17506402983406999276)
XLA Ops:
  0.6 14.7 %shard_map.86 = (f32[3,32,128]{2,1,0:T(8,128)S(1)}, f32[32,128]{1,0:T(8,128)S(1)}) custom-call(bf16[32,128,128]{2,1,0:T(8,128)(2,1)} %field.1, s32[1,4,4]{2,1,0:T(4,128)} %live_in.1, s32[16,16]{1,0:T(8,128)} %order_in.1, f32[4]{0:T(128)} %centers_in.1, f32[4]{0:T(128)} %widths_in.1, f32[4]{0:T(128)} %heights_in.1, f32[4,3]{1,0:T(4,128)} %colours_in.1), custom_call_target="tpu_custom_call" | custom-call | tf_op jit(solution)/shard_map/pallas_call | solution.py:317
  15.4 0.6 %copy.11 = f32[3,32,128]{2,1,0:T(8,128)} copy(f32[3,32,128]{2,1,0:T(8,128)S(1)} %get-tuple-element.2) | data formatting | bytes 98304
  16.0 0.6 %copy.12 = f32[32,128]{1,0:T(8,128)} copy(f32[32,128]{1,0:T(8,128)S(1)} %get-tuple-element.3) | data formatting | bytes 32768
